TPU v7x, 256 devices: a whole 4x4x8 slice. The times are simulated.
256 devices in a mesh: grp: 8 (over x, y_lo), wide: 32 (over y_hi, z, core).
Axes of the slice: x: 4, y: 4 (y_hi: 2, y_lo: 2; y = y_hi * 2 + y_lo), z: 8, core: 2. Of those that a mesh axis runs over, the one named last changes fastest.
Arguments:
- src_rows: float32 [262144, 400], P(('grp', 'wide')), may hold values from -16 to 16
- src_accum: float32 [262144], P(('grp', 'wide')), may hold values from 0.1 to 4
- dst_rows: float32 [16384, 400], P(('grp', 'wide')), may hold values from -1.5 to 1.5
- dst_accum: float32 [16384], P(('grp', 'wide')), may hold values from 0.1 to 4
- relations: float32 [1024, 400], replicated, may hold values from -4 to 4
- rel_ids: int32 [2, 262144], P(None, ('grp', 'wide')), may hold values from 0 to 1023
- targets: int32 [2, 262144], P(None, ('grp', 'wide')), may hold values from 0 to 2047
Outputs:
- new_src: float32 [262144, 400], P(('grp', 'wide'))
- new_src_accum: float32 [262144], P(('grp', 'wide'))
- new_dst: float32 [16384, 400], P(('grp', 'wide'))
- new_dst_accum: float32 [16384], P(('grp', 'wide'))
- edge_loss: float32 [2, 262144], P(None, ('grp', 'wide'))
All inputs are finite; a program needn't handle non-finite values.
Results may differ from a plain program's by a relative error of at most 0.009.
Values may be sent and summed in bfloat16 or wider, within the bound.
A program may use at most 64 MiB of HBM per device.

v0:
```python
import jax
import jax.numpy as jnp
from jax import lax
from jax.sharding import PartitionSpec as P

ROUNDS = 2
LEARN_RATE = 0.1


def passed_along(block, axis, distance):
    devices = range(lax.axis_size(axis))
    route = [((i - distance) % len(devices), i) for i in devices]
    return lax.ppermute(block, axis, route)


def adagrad(table_rows, accumulator, gradients):
    accumulator = accumulator + jnp.mean(gradients * gradients, axis=-1)
    return (table_rows - LEARN_RATE * gradients / jnp.sqrt(accumulator)[..., None], accumulator)


def score_blocks(key_rows, query_rows, label_ids):
    src_count, feat_width = query_rows.shape
    block_rows = 512
    block_count = src_count // block_rows

    def visit(running, pieces):
        query, labels = pieces
        logits = jnp.einsum("sd,bd->sb", query, key_rows, preferred_element_type=jnp.float32)
        top_score = jnp.max(logits, axis=1, keepdims=True)
        exp_scores = jnp.exp(logits - top_score)
        exp_total = jnp.sum(exp_scores, axis=1, keepdims=True)
        target_hit = lax.broadcasted_iota(jnp.int32, logits.shape, 1) == labels[:, None]
        picked = jnp.sum(jnp.where(target_hit, logits, 0.0), axis=1)
        losses = top_score[:, 0] + jnp.log(exp_total[:, 0]) - picked
        residual = (exp_scores / exp_total - target_hit.astype(jnp.float32)).astype(jnp.bfloat16)
        grad_query = jnp.dot(residual, key_rows, preferred_element_type=jnp.float32)
        running = running + jnp.einsum(
            "sb,sd->bd", residual, query, preferred_element_type=jnp.float32
        )
        return (running, (losses, grad_query))

    pieces = (
        query_rows.reshape(block_count, block_rows, feat_width),
        label_ids.reshape(block_count, block_rows),
    )
    zeros = jnp.zeros((key_rows.shape[0], feat_width), jnp.float32)
    running, outputs = lax.scan(visit, zeros, pieces)
    losses, grad_query = outputs
    return (losses.reshape(src_count), grad_query.reshape(src_count, feat_width), running)


def shards(src_rows, src_accum, dst_rows, dst_accum, relations, rel_ids, targets):
    loss_list = []
    for round_index in range(ROUNDS):
        key_rows = lax.all_gather(dst_rows.astype(jnp.bfloat16), "wide", axis=0, tiled=True)
        rel_scales = jnp.take(relations, rel_ids[round_index], axis=0)
        query_rows = (src_rows * rel_scales).astype(jnp.bfloat16)
        label_ids = targets[round_index]
        losses, grad_query, partial_value = score_blocks(key_rows, query_rows, label_ids)
        grad_dst = lax.psum_scatter(
            partial_value.astype(jnp.bfloat16), "wide", scatter_dimension=0, tiled=True
        ).astype(jnp.float32)
        src_rows, src_accum = adagrad(src_rows, src_accum, grad_query * rel_scales)
        dst_rows, dst_accum = adagrad(dst_rows, dst_accum, grad_dst)
        loss_list.append(losses)
        if round_index + 1 < ROUNDS:
            dst_rows, dst_accum = passed_along((dst_rows, dst_accum), "grp", 1)
    return (src_rows, src_accum, dst_rows, dst_accum, jnp.stack(loss_list))


def solution(mesh):
    placed = (
        P(("grp", "wide"), None),
        P(("grp", "wide")),
        P(("grp", "wide"), None),
        P(("grp", "wide")),
        P(),
        P(None, ("grp", "wide")),
        P(None, ("grp", "wide")),
    )
    return jax.shard_map(
        shards,
        mesh=mesh,
        in_specs=placed,
        out_specs=(
            P(("grp", "wide"), None),
            P(("grp", "wide")),
            P(("grp", "wide"), None),
            P(("grp", "wide")),
            P(None, ("grp", "wide")),
        ),
        check_vma=False,
    )
```

profile of v0, /device:TPU:2, one launch (start us, length us, event | category | flops | bytes accessed | tf_op | source)
XLA Modules:
  0.0 495.0 jit_solution(9824283437279981220)
XLA Ops:
  7.2 1.5 convert_element_type.37
  8.8 1.8 copy.31
  10.7 2.8 copy.34
  13.6 4.9 gather_fusion
  18.5 2.5 multiply_convert_fusion.1
  21.0 73.1 %all-gather.3.cloned.1.call-done = bf16[2048,400]{1,0:T(8,128)(2,1)} async-done(((bf16[64,400]{1,0:T(8,128)(2,1)}), bf16[2048,400]{1,0:T(8,128)(2,1)}) %all-gather.3.cloned.1.call-update) | async-done | bytes 1638416 | tf_op jit(solution)/shard_map/all_gather | solution.py:55
  94.2 1.4 broadcast.38.clone
  95.5 31.9 %while.30 = (s32[]{:T(128)}, f32[2048,400]{0,1:T(8,128)}, f32[2,512]{1,0:T(2,128)S(1)}, f32[2,512,400]{1,2,0:T(8,128)}, bf16[2,512,400]{2,1,0:T(8,128)(2,1)S(1)}...) while((s32[]{:T(128)}, f32[2048,400]{0,1:T(8,128)}, ...), condition=%wide.region_4.6_spmd.clone, body=%wide.region_0.5_spmd.clone.sunk | while | flops 2530803200 | bytes 31064192 | solution.py:47
  95.5 3.0 fusion.60
  98.5 1.4 select_reduce_fusion.4
  99.9 2.5 subtract_convert_fusion.4
  102.4 4.3 select_add_fusion.4
  106.8 4.2 fusion.61
  111.0 3.0 fusion.60
  114.0 1.4 select_reduce_fusion.4
  115.4 2.5 subtract_convert_fusion.4
  117.9 5.3 %select_add_fusion.4 = f32[2048,400]{0,1:T(8,128)} fusion(f32[2048,400]{0,1:T(8,128)} %get-tuple-element.322, bf16[512,2048]{1,0:T(8,128)(2,1)} %subtract_convert_fusion.4, pred[]{:T(512)S(6)} %compare.6, bf16[2,512,400]{2,1,0:T(8,128)(2,1)S(1)} %get-tuple-element.334, s32[]{:T(128)S(6)} %copy.55), kind=kOutput, calls=%fused_computation.7.clone.1 | convolution fusion | flops 840499200 | bytes 9175045 | tf_op jit(solution)/shard_map/while/body/eval_jaxpr/sb,sd->bd/dot_general | solution.py:37
  123.3 4.2 fusion.61
  127.4 3.4 convert_element_type.39
  130.9 3.8 copy.41
  134.9 116.2 %reduce-scatter.7.cloned.1.call-done = bf16[64,400]{1,0:T(8,128)(2,1)} async-done(((bf16[2048,400]{1,0:T(8,128)(2,1)}), bf16[64,400]{1,0:T(8,128)(2,1)}) %reduce-scatter.7.cloned.1.call-update) | async-done | bytes 51216
  251.1 1.0 copy.42
  252.9 6.1 %collective-permute-done = f32[64,400]{0,1:T(8,128)S(1)} collective-permute-done((f32[64,400]{0,1:T(8,128)S(1)}, f32[64,400]{0,1:T(8,128)S(1)}, u32[]{:S(2)}, u32[]{:S(2)}) %collective-permute-start) | collective-permute-done | bytes 102432 | tf_op jit(solution)/shard_map/ppermute | solution.py:13
  259.9 4.9 gather_fusion.1
  264.9 3.0 copy.33
  268.0 2.2 multiply_reduce_fusion.1
  270.9 3.3 multiply_convert_fusion
  274.1 63.0 %all-gather.5.cloned.1.call-done = bf16[2048,400]{1,0:T(8,128)(2,1)} async-done(((bf16[64,400]{1,0:T(8,128)(2,1)}), bf16[2048,400]{1,0:T(8,128)(2,1)}) %all-gather.5.cloned.1.call-update) | async-done | bytes 1638416 | tf_op jit(solution)/shard_map/all_gather | solution.py:55
  337.1 1.4 broadcast.38
  338.5 26.5 %while.31 = (s32[]{:T(128)}, f32[2048,400]{0,1:T(8,128)}, f32[2,512]{1,0:T(2,128)S(1)}, f32[2,512,400]{1,2,0:T(8,128)}, bf16[2,512,400]{2,1,0:T(8,128)(2,1)S(1)}...) while((s32[]{:T(128)}, f32[2048,400]{0,1:T(8,128)}, ...), condition=%wide.region_12.14_spmd.clone, body=%wide.region_8.13_spmd.clone.sunk | while | flops 2530803200 | bytes 31064192 | solution.py:47
  338.5 3.0 fusion.67
  341.5 1.4 select_reduce_fusion.5
  342.9 1.6 subtract_convert_fusion.5
  344.5 2.8 select_add_fusion.5
  347.3 3.5 fusion.68
  350.8 3.0 fusion.67
  353.8 1.4 select_reduce_fusion.5
  355.2 1.6 subtract_convert_fusion.5
  356.8 4.7 select_add_fusion.5
  361.5 3.5 fusion.68
  365.0 2.2 convert_element_type.42
  367.2 2.4 copy.43
  370.3 2.9 copy.38
  373.2 2.2 multiply_reduce_fusion
  376.1 1.8 divide_subtract_fusion
  377.9 2.8 copy.39
  381.3 104.8 %reduce-scatter.9.cloned.1.call-done = bf16[64,400]{1,0:T(8,128)(2,1)} async-done(((bf16[2048,400]{1,0:T(8,128)(2,1)}), bf16[64,400]{1,0:T(8,128)(2,1)}) %reduce-scatter.9.cloned.1.call-update) | async-done | bytes 51216
  486.1 1.0 copy.44
  (71 shorter events, 6.3 us)
Async XLA Ops:
  7.2 87.0 %all-gather.3.cloned.1.call-start = ((), (), s32[]{:S(2)}) async-start(), calls=%async_computation.2 | async-start | bytes 2162688 | tf_op jit(solution)/shard_map/all_gather | solution.py:55
  8.8 242.3 %reduce-scatter.7.cloned.1.call-start = ((), (), s32[]{:S(2)}) async-start(), calls=%async_computation.4 | async-start | bytes 2162688
  10.7 2.9 copy-start.8
  10.7 2.9 copy-start.9
  130.9 3.9 copy-start.6
  134.7 117.5 %copy-start.10 = (f32[64]{0:T(128)S(1)}, f32[64]{0:T(128)}, u32[]{:S(2)}) copy-start(f32[64]{0:T(128)} %param.16) | copy-start | bytes 772
  134.7 202.4 %all-gather.5.cloned.1.call-start = ((), (), s32[]{:S(2)}) async-start(), calls=%async_computation.3 | async-start | bytes 2162688 | tf_op jit(solution)/shard_map/all_gather | solution.py:55
  252.2 6.7 %collective-permute-start = (f32[64,400]{0,1:T(8,128)S(1)}, f32[64,400]{0,1:T(8,128)S(1)}, u32[]{:S(2)}, u32[]{:S(2)}) collective-permute-start(f32[64,400]{0,1:T(8,128)S(1)} %fusion.19), channel_id=1, source_target_pairs={{224,0},{0,32},{32,64},{64,96},{96,128},{128,160},{160,192},{192,2... | collective-permute-start | bytes 307208 | tf_op jit(solution)/shard_map/ppermute | solution.py:13
  259.7 226.4 %reduce-scatter.9.cloned.1.call-start = ((), (), s32[]{:S(2)}) async-start(), calls=%async_computation.5 | async-start | bytes 2162688
  264.9 3.1 copy-start
  267.9 2.3 copy-start.7
  267.9 2.3 copy-start.1
  267.9 2.9 copy-start.3
  369.7 3.5 copy-start.2
  369.7 117.4 %collective-permute-start.1 = (f32[64]{0:T(128)S(1)}, f32[64]{0:T(128)S(1)}, u32[]{:S(2)}, u32[]{:S(2)}) collective-permute-start(f32[64]{0:T(128)S(1)} %get-tuple-element.199), channel_id=1, source_target_pairs={{224,0},{0,32},{32,64},{64,96},{96,128},{128,160},{160,192},{192,2... | collective-permute-start | bytes 776 | tf_op jit(solution)/shard_map/ppermute | solution.py:13
  373.2 2.8 copy-start.4
  373.2 2.9 copy-start.5
Sparse Core Ops, SparseCore 0:
  11.3 82.7 all-gather.2
  134.8 116.2 reduce-scatter.6
  259.8 77.2 all-gather.4
  369.8 116.2 reduce-scatter.8
where the time goes:
time: 496 us; the launch traced here: 495 us
  waiting for transfers between devices  363 us (73%)
  matrix products  44.4 us (9%)
  local copies, waits for them, and re-layouts  36.6 us (7%)
  other arithmetic  35 us (7%)
  between operations  14 us (3%)
    unnamed x6, waiting for transfers between devices  221 us
    all_gather x2, waiting for transfers between devices, shards(): lax.all_gather(dst_rows.astype(jnp.bfloat16), 'wide', axis=0, tiled=True)  136 us
    unnamed x33, local copies, waits for them, and re-layouts  17.2 us
    dot_general x4, matrix products, visit(): jnp.einsum('sb,sd->bd', residual, query, preferred_element_type=jnp.float32)  17.1 us
    dot_general x4, matrix products, visit(): grad_query = jnp.dot(residual, key_rows, preferred_element_type=jnp.float32)  15.5 us
    dot_general x4, matrix products, visit(): jnp.einsum('sd,bd->sb', query, key_rows, preferred_element_type=jnp.float32)  11.8 us
  transfers between devices with their start and end apart: 6, of which 5 were waited for; matrix products, arithmetic and copies ran while one was open for 8% of the time, Pallas kernels for 0%

commit v1 on v0

--- a/solution.py
+++ b/solution.py
@@ -52,7 +52,12 @@
 def shards(src_rows, src_accum, dst_rows, dst_accum, relations, rel_ids, targets):
     loss_list = []
     for round_index in range(ROUNDS):
-        key_rows = lax.all_gather(dst_rows.astype(jnp.bfloat16), "wide", axis=0, tiled=True)
+        key_rows = jnp.concatenate(
+            lax.all_to_all(
+                jnp.stack([dst_rows.astype(jnp.bfloat16)] * lax.axis_size("wide")), "wide", 0, 0
+            ),
+            axis=0,
+        )
         rel_scales = jnp.take(relations, rel_ids[round_index], axis=0)
         query_rows = (src_rows * rel_scales).astype(jnp.bfloat16)
         label_ids = targets[round_index]

time: 496 us -> 456 us (0.919)
  waiting for transfers between devices: 363 us -> 303 us
  starting transfers between devices: 1.67 us -> 19.4 us
    all_gather x2 -> x0, waiting for transfers between devices: 136 us -> none  [shards(): lax.all_gather(dst_rows.astype(jnp.bfloat16), 'wide', axis=0, tiled=True)]
    all_to_all x0 -> x2, waiting for transfers between devices: none -> 77.1 us  [shards(): lax.all_to_all(jnp.stack([dst_rows.astype(jnp.bfloat16)] * lax.axis_size(...]
    all_to_all x0 -> x2, starting transfers between devices: none -> 17.8 us  [shards(): lax.all_to_all(jnp.stack([dst_rows.astype(jnp.bfloat16)] * lax.axis_size(...]
    unnamed x6 -> x4, waiting for transfers between devices: 221 us -> 220 us
where the time goes in v1:
time: 456 us; the launch traced here: 455 us
  waiting for transfers between devices  303 us (66%)
  matrix products  44.4 us (10%)
  local copies, waits for them, and re-layouts  39.1 us (9%)
  other arithmetic  34.3 us (8%)
  starting transfers between devices  19.4 us (4%)
  between operations  14.3 us (3%)
    unnamed x4, waiting for transfers between devices  220 us
    all_to_all x2, waiting for transfers between devices, shards(): lax.all_to_all(jnp.stack([dst_rows.astype(jnp.bfloat16)] * lax.axis_size(...  77.1 us
    all_to_all x2, starting transfers between devices, shards(): lax.all_to_all(jnp.stack([dst_rows.astype(jnp.bfloat16)] * lax.axis_size(...  17.8 us
    unnamed x33, local copies, waits for them, and re-layouts  17.2 us
    dot_general x4, matrix products, visit(): jnp.einsum('sb,sd->bd', residual, query, preferred_element_type=jnp.float32)  17.1 us
    dot_general x4, matrix products, visit(): grad_query = jnp.dot(residual, key_rows, preferred_element_type=jnp.float32)  15.5 us
    dot_general x4, matrix products, visit(): jnp.einsum('sd,bd->sb', query, key_rows, preferred_element_type=jnp.float32)  11.8 us
    gather x2, local copies, waits for them, and re-layouts, shards(): rel_scales = jnp.take(relations, rel_ids[round_index], axis=0)  9.8 us
  transfers between devices with their start and end apart: 6, of which 5 were waited for; matrix products, arithmetic and copies ran while one was open for 8% of the time, Pallas kernels for 0%

profile of v1, /device:TPU:2, one launch (start us, length us, event | category | flops | bytes accessed | tf_op | source)
XLA Modules:
  0.0 455.0 jit_solution(15477853959088115230)
XLA Ops:
  8.1 1.6 stack.6
  9.6 11.6 %all-to-all-start = ((bf16[32,64,400]{2,1,0:T(8,128)(2,1)}), bf16[32,64,400]{2,1,0:T(8,128)(2,1)}, u32[]{:S(2)}, u32[]{:S(2)}) async-start(bf16[32,64,400]{2,1,0:T(8,128)(2,1)} %stack.6), calls=%async_computation | async-start | bytes 4194304 | tf_op jit(solution)/shard_map/all_to_all | solution.py:56
  21.3 1.8 copy.31
  23.2 2.8 copy.34
  26.1 4.9 %gather_fusion = f32[1024,400]{1,0:T(8,128)} fusion(f32[1024,400]{1,0:T(8,128)S(1)} %copy.31, s32[1024]{0:T(1024)S(1)} %fusion.24), kind=kCustom, calls=%fused_computation.clone | custom fusion | bytes 3280896 | tf_op jit(solution)/shard_map/jit(_take)/gather | solution.py:61
  31.0 2.5 multiply_convert_fusion.1
  33.5 39.6 %all-to-all-done = bf16[32,64,400]{2,1,0:T(8,128)(2,1)} async-done(((bf16[32,64,400]{2,1,0:T(8,128)(2,1)}), bf16[32,64,400]{2,1,0:T(8,128)(2,1)}, u32[]{:S(2)}, u32[]{:S(2)}) %all-to-all-start) | async-done | bytes 1638432 | tf_op jit(solution)/shard_map/all_to_all | solution.py:56
  73.1 1.4 broadcast.42.clone
  74.5 31.9 %while.30 = (s32[]{:T(128)}, f32[2048,400]{0,1:T(8,128)}, f32[2,512]{1,0:T(2,128)S(1)}, f32[2,512,400]{1,2,0:T(8,128)}, bf16[2,512,400]{2,1,0:T(8,128)(2,1)S(1)}...) while((s32[]{:T(128)}, f32[2048,400]{0,1:T(8,128)}, ...), condition=%wide.region_4.6_spmd.clone, body=%wide.region_0.5_spmd.clone.sunk | while | flops 2530803200 | bytes 31064192 | solution.py:47
  74.5 3.0 fusion.60
  77.4 1.4 select_reduce_fusion.4
  78.9 2.5 subtract_convert_fusion.4
  81.4 4.4 select_add_fusion.4
  85.8 4.2 fusion.61
  90.0 3.0 fusion.60
  92.9 1.4 select_reduce_fusion.4
  94.3 2.5 subtract_convert_fusion.4
  96.9 5.3 %select_add_fusion.4 = f32[2048,400]{0,1:T(8,128)} fusion(f32[2048,400]{0,1:T(8,128)} %get-tuple-element.315, bf16[512,2048]{1,0:T(8,128)(2,1)} %subtract_convert_fusion.4, pred[]{:T(512)S(6)} %compare.6, bf16[2,512,400]{2,1,0:T(8,128)(2,1)S(1)} %get-tuple-element.327, s32[]{:T(128)S(6)} %copy.55), kind=kOutput, calls=%fused_computation.7.clone.1 | convolution fusion | flops 840499200 | bytes 9175045 | tf_op jit(solution)/shard_map/while/body/eval_jaxpr/sb,sd->bd/dot_general | solution.py:37
  102.2 4.2 fusion.61
  106.4 3.4 convert_element_type.39
  109.8 3.8 copy.41
  113.8 116.0 %reduce-scatter.7.cloned.1.call-done = bf16[64,400]{1,0:T(8,128)(2,1)} async-done(((bf16[2048,400]{1,0:T(8,128)(2,1)}), bf16[64,400]{1,0:T(8,128)(2,1)}) %reduce-scatter.7.cloned.1.call-update) | async-done | bytes 51216
  231.6 6.0 %collective-permute-done = f32[64,400]{0,1:T(8,128)S(1)} collective-permute-done((f32[64,400]{0,1:T(8,128)S(1)}, f32[64,400]{0,1:T(8,128)S(1)}, u32[]{:S(2)}, u32[]{:S(2)}) %collective-permute-start) | collective-permute-done | bytes 102432 | tf_op jit(solution)/shard_map/ppermute | solution.py:13
  237.7 1.7 stack.7
  239.4 6.1 %all-to-all-start.1 = ((bf16[32,64,400]{2,1,0:T(8,128)(2,1)}), bf16[32,64,400]{2,1,0:T(8,128)(2,1)}, u32[]{:S(2)}, u32[]{:S(2)}) async-start(bf16[32,64,400]{2,1,0:T(8,128)(2,1)} %stack.7), calls=%async_computation.1 | async-start | bytes 4194304 | tf_op jit(solution)/shard_map/all_to_all | solution.py:56
  245.8 4.9 %gather_fusion.1 = f32[1024,400]{1,0:T(8,128)} fusion(f32[1024,400]{1,0:T(8,128)S(1)} %copy.31, s32[1024]{0:T(1024)S(1)} %fusion.25), kind=kCustom, calls=%fused_computation.1.clone | custom fusion | bytes 3280896 | tf_op jit(solution)/shard_map/jit(_take)/gather | solution.py:61
  250.7 3.0 copy.33
  253.7 2.2 multiply_reduce_fusion.1
  256.5 3.3 multiply_convert_fusion
  259.8 37.5 %all-to-all-done.1 = bf16[32,64,400]{2,1,0:T(8,128)(2,1)} async-done(((bf16[32,64,400]{2,1,0:T(8,128)(2,1)}), bf16[32,64,400]{2,1,0:T(8,128)(2,1)}, u32[]{:S(2)}, u32[]{:S(2)}) %all-to-all-start.1) | async-done | bytes 1638432 | tf_op jit(solution)/shard_map/all_to_all | solution.py:56
  298.7 26.5 %while.31 = (s32[]{:T(128)}, f32[2048,400]{0,1:T(8,128)}, f32[2,512]{1,0:T(2,128)S(1)}, f32[2,512,400]{1,2,0:T(8,128)}, bf16[2,512,400]{2,1,0:T(8,128)(2,1)S(1)}...) while((s32[]{:T(128)}, f32[2048,400]{0,1:T(8,128)}, ...), condition=%wide.region_12.14_spmd.clone, body=%wide.region_8.13_spmd.clone.sunk | while | flops 2530803200 | bytes 31064192 | solution.py:47
  298.7 3.0 fusion.67
  301.7 1.4 select_reduce_fusion.5
  303.1 1.6 subtract_convert_fusion.5
  304.7 2.8 select_add_fusion.5
  307.5 3.5 fusion.68
  311.0 3.0 fusion.67
  314.0 1.4 select_reduce_fusion.5
  315.4 1.6 subtract_convert_fusion.5
  317.0 4.7 %select_add_fusion.5 = f32[2048,400]{0,1:T(8,128)} fusion(f32[2048,400]{0,1:T(8,128)} %get-tuple-element.342, bf16[512,2048]{1,0:T(8,128)(2,1)S(1)} %subtract_convert_fusion.5, pred[]{:T(512)S(6)} %compare.7, bf16[2,512,400]{2,1,0:T(8,128)(2,1)S(1)} %get-tuple-element.354, s32[]{:T(128)S(6)} %copy.67), kind=kOutput, calls=%fused_computation.24.clone.1 | convolution fusion | flops 840499200 | bytes 9175045 | tf_op jit(solution)/shard_map/while/body/eval_jaxpr/sb,sd->bd/dot_general | solution.py:37
  321.7 3.5 fusion.68
  325.3 2.2 convert_element_type.42
  327.4 2.4 copy.43
  330.5 2.9 copy.38
  333.4 2.2 multiply_reduce_fusion
  336.2 1.8 divide_subtract_fusion
  338.1 2.8 copy.39
  341.4 104.3 %reduce-scatter.9.cloned.1.call-done = bf16[64,400]{1,0:T(8,128)(2,1)} async-done(((bf16[2048,400]{1,0:T(8,128)(2,1)}), bf16[64,400]{1,0:T(8,128)(2,1)}) %reduce-scatter.9.cloned.1.call-update) | async-done | bytes 51216
  (71 shorter events, 9.7 us)
Async XLA Ops:
  9.6 63.5 %all-to-all-start = ((bf16[32,64,400]{2,1,0:T(8,128)(2,1)}), bf16[32,64,400]{2,1,0:T(8,128)(2,1)}, u32[]{:S(2)}, u32[]{:S(2)}) async-start(bf16[32,64,400]{2,1,0:T(8,128)(2,1)} %stack.6), calls=%async_computation | async-start | bytes 4194304 | tf_op jit(solution)/shard_map/all_to_all | solution.py:56
  21.3 208.5 %reduce-scatter.7.cloned.1.call-start = ((), (), s32[]{:S(2)}) async-start(), calls=%async_computation.4 | async-start | bytes 2162688
  23.2 2.9 copy-start.8
  23.2 2.9 copy-start.9
  109.8 3.8 copy-start.6
  113.6 117.2 %copy-start.10 = (f32[64]{0:T(128)S(1)}, f32[64]{0:T(128)}, u32[]{:S(2)}) copy-start(f32[64]{0:T(128)} %param.16) | copy-start | bytes 772
  230.9 6.7 %collective-permute-start = (f32[64,400]{0,1:T(8,128)S(1)}, f32[64,400]{0,1:T(8,128)S(1)}, u32[]{:S(2)}, u32[]{:S(2)}) collective-permute-start(f32[64,400]{0,1:T(8,128)S(1)} %fusion.19), channel_id=1, source_target_pairs={{224,0},{0,32},{32,64},{64,96},{96,128},{128,160},{160,192},{192,2... | collective-permute-start | bytes 307208 | tf_op jit(solution)/shard_map/ppermute | solution.py:13
  239.4 58.0 %all-to-all-start.1 = ((bf16[32,64,400]{2,1,0:T(8,128)(2,1)}), bf16[32,64,400]{2,1,0:T(8,128)(2,1)}, u32[]{:S(2)}, u32[]{:S(2)}) async-start(bf16[32,64,400]{2,1,0:T(8,128)(2,1)} %stack.7), calls=%async_computation.1 | async-start | bytes 4194304 | tf_op jit(solution)/shard_map/all_to_all | solution.py:56
  245.5 200.3 %reduce-scatter.9.cloned.1.call-start = ((), (), s32[]{:S(2)}) async-start(), calls=%async_computation.5 | async-start | bytes 2162688
  250.7 3.0 copy-start
  253.7 2.2 copy-start.7
  253.7 2.3 copy-start.1
  253.7 2.9 copy-start.3
  329.9 3.5 copy-start.2
  329.9 116.9 %collective-permute-start.1 = (f32[64]{0:T(128)S(1)}, f32[64]{0:T(128)S(1)}, u32[]{:S(2)}, u32[]{:S(2)}) collective-permute-start(f32[64]{0:T(128)S(1)} %get-tuple-element.192), channel_id=1, source_target_pairs={{224,0},{0,32},{32,64},{64,96},{96,128},{128,160},{160,192},{192,2... | collective-permute-start | bytes 776 | tf_op jit(solution)/shard_map/ppermute | solution.py:13
  333.4 2.8 copy-start.4
  333.4 2.9 copy-start.5
Sparse Core Ops, SparseCore 0:
  113.8 115.9 reduce-scatter.6
  330.0 115.7 reduce-scatter.8
